TPU v7x, 32 devices: a whole 2x2x4 slice. The times are simulated.
32 devices in a mesh: tm: 4 (over y, x), space: 8 (over z, core).
Axes of the slice: x: 2, y: 2, z: 4, core: 2. Of those that a mesh axis runs over, the one named last changes fastest.
Arguments:
- ckpt_store: float32 [4, 8, 8, 5120], P('tm', 'space'), may hold values from -6 to 6
- ckpt_target: int32 [4, 8, 8], P('tm'), may hold values from 0 to 7, as said below
- ckpt_block: int32 [4, 8, 8], P('tm'), may hold values from 0 to 7, as said below
- lengths: int32 [4], replicated, may hold values from 1 to 3, 8 in all
- obs_adjoint: float32 [4, 5, 32, 16, 128], P('tm', None, 'space'), may hold values from -6 to 6
- w_in: bfloat16 [16, 135], replicated, may hold values from -0.5 to 0.5
- w_out: bfloat16 [5, 16], replicated, may hold values from -1.5 to 1.5
Outputs:
- start_adjoint: float32 [4, 5, 32, 16, 128], P('tm', None, 'space')
- grad_in: float32 [16, 135], replicated
- grad_out: float32 [5, 16], replicated
Inputs may be any that keep to these rules, and one draw needn't show every extreme that they name: In each section every block b of every slab p is stored in exactly one holder and slot, with ckpt_target = p and ckpt_block = b there. One holder stores at most 2 blocks of one slab in a section, and exactly 2 of some. `ckpt_block`: within a section and target slab, the block indices are all different.
All inputs are finite; a program needn't handle non-finite values.
Results may differ from a plain program's by a relative error of at most 0.0083.
Values sent between devices are 32-bit elements; how exact they have to be, the bound alone decides.
A program may use at most 64 MiB of HBM per device.

v0:
```python
import functools
import math

import jax
import jax.numpy as jnp
from jax import lax
from jax.experimental import pallas as pl
from jax.experimental.pallas import tpu as pltpu
from jax.sharding import PartitionSpec as P

SEC_MOST = 3
DT = 0.08
MESH = pl.DeviceIdType.MESH
F32 = jnp.float32
BF16 = jnp.bfloat16


def table_kernel(slabs, targets_ref, blocks_ref, table_ref):
    me = lax.axis_index("space")

    def holder(h, _):
        def slot(j, count):
            mine = targets_ref[h, j] == me

            @pl.when(mine)
            def _():
                table_ref[blocks_ref[h, j]] = 2 * h + count

            return count + jnp.where(mine, 1, 0)

        lax.fori_loop(0, slabs, slot, 0)
        return 0

    lax.fori_loop(0, slabs, holder, 0)


def picks(shape, axis, middle, last, fields):
    j = lax.broadcasted_iota(jnp.int32, shape, axis)
    i = lax.broadcasted_iota(jnp.int32, shape, 1 - axis)
    outer = jnp.where(j >= 24, 1, 0) + jnp.where(j >= 48, 1, 0)
    inner = (j >> 3) - 3 * outer
    f = j & 7
    source = (9 * outer + middle * inner + last) * fields + f
    return jnp.logical_and(jnp.logical_and(f < fields, j < 72), i == source)


def finish_kernel(state_ref, sums_ref, out_ref, gin_ref, gout_ref):
    planes, ny, fields = state_ref.shape[:3]
    for q in range(planes):
        for y in range(ny):
            for f in range(fields):
                out_ref[f, q, y : y + 1, :] = state_ref[q, y, f : f + 1, :]
    taps_all = gin_ref.shape[1]
    total_in = jnp.zeros((16, taps_all), F32)
    for c in range(3):
        sel = jnp.where(picks((80, taps_all), 0, 3, c, fields), 1.0, 0.0)
        total_in = total_in + jnp.dot(
            sums_ref[16 * c : 16 * c + 16, 0:80], sel, precision=lax.Precision.HIGHEST,
            preferred_element_type=F32,
        )
    gin_ref[...] = total_in
    gout_ref[...] = sums_ref[48 : 48 + fields, 0:16]


def main_kernel(
    dims,
    store, targets, blocks, given, lengths, obs_in, w_in, w_out,
    out_ref, gfin,
    outgoing, obs, table,
    arrived, full, stc, obsr, taps, dh, hl, pd, gl, blp, own, hist, sendp, sendm, recvp, recvm,
    osend, u_ref, c_ref, wf, wc, wo, wot, pin_ref, pout_ref, gpart, g1, g2, g3,
    a2a_s, a2a_r, init_s, init_r, obs_s, obs_r, fwd_s, fwd_r, ch_s, ch_r, out_s, out_r, loc, r1_s, r1_r, r2_s, r2_r, r3_s, r3_r, pair_s, pair_r,
):
    sections, slabs, planes, ny, fields, rows, steps, scale = dims
    t = lax.axis_index("tm")
    p = lax.axis_index("space")
    nx = slabs * planes

    def gray(r):
        return r + (r // 2) * (1 - 2 * (r % 2))

    def flip(pp, i):
        return i + (pp % 2) * (planes - 1 - 2 * i)

    def device_of(x):
        pair = x // (2 * planes)
        i = x % (2 * planes)
        return gray(flip(pair, i // 2)), 2 * pair + i % 2

    active = t < planes
    x = (p // 2) * 2 * planes + 2 * flip(p // 2, gray(t)) + p % 2
    home, spot = x // planes, x % planes

    def rcopy(src, dst, ss, rs, tt, pp):
        return pltpu.make_async_remote_copy(
            src_ref=src, dst_ref=dst, send_sem=ss, recv_sem=rs,
            device_id={"tm": tt, "space": pp}, device_id_type=MESH,
        )

    barrier = pltpu.get_barrier_semaphore()
    total = sections * slabs
    mine = t * slabs + p

    def greet(j, _):
        other = (mine + j) % total
        there, slab = other // slabs, other % slabs
        gap = slab // 2 - p // 2
        near = jnp.logical_and(gap >= -1, gap <= 1)

        @pl.when(jnp.logical_or(there == t, near))
        def _():
            pl.semaphore_signal(
                barrier, inc=1, device_id={"tm": there, "space": slab}, device_id_type=MESH
            )

        return 0

    lax.fori_loop(1, total, greet, 0)

    def group(q, _):
        def slot(j, found):
            count, one, two = found
            hit = targets[p, j] == q
            one = jnp.where(jnp.logical_and(hit, count == 0), j, one)
            two = jnp.where(jnp.logical_and(hit, count == 1), j, two)
            return count + jnp.where(hit, 1, 0), one, two

        zero = jnp.int32(0)
        if slabs <= 16:
            found = (zero, zero, zero)
            for j in range(slabs):
                found = slot(j, found)
        else:
            found = lax.fori_loop(0, slabs, slot, (zero, zero, zero))
        for rank in range(2):
            line = store[pl.ds(found[1 + rank], 1), :]
            for k in range(rows):
                outgoing[q, rank, pl.ds(k, 1), :] = line[:, k * 128 : (k + 1) * 128]
        return 0

    lax.fori_loop(0, slabs, group, 0)
    for q in range(planes):
        for y in range(ny):
            for f in range(fields):
                obs[q, y, f : f + 1, :] = obs_in[f, q, y : y + 1, :]
    beside = 1 + jnp.where(p // 2 > 0, 1, 0) + jnp.where(p // 2 < slabs // 2 - 1, 1, 0)
    pl.semaphore_wait(barrier, slabs - 1 + (sections - 1) * 2 * beside)

    def a2a(peer):
        return rcopy(outgoing.at[peer], arrived.at[p], a2a_s.at[peer], a2a_r.at[p], t, peer)

    def a2a_start(j, _):
        far = slabs - j

        @pl.when(p + far < slabs)
        def _():
            a2a(p + far).start()

        @pl.when(p >= far)
        def _():
            a2a(p - far).start()

        return 0

    lax.fori_loop(1, slabs, a2a_start, 0)
    keep = pltpu.make_async_copy(outgoing.at[p], arrived.at[p], loc.at[0])
    keep.start()

    def each_obs(q, action):
        tt, pp = device_of(p * planes + q)
        same = jnp.logical_and(tt == t, pp == p)

        @pl.when(jnp.logical_not(same))
        def _():
            action(rcopy(obs.at[q], obsr.at[t], obs_s.at[q], obs_r.at[t], tt, pp), False)

        @pl.when(same)
        def _():
            action(pltpu.make_async_copy(obs.at[q], obsr.at[t], loc.at[1]), True)

    for q in range(planes):
        each_obs(q, lambda c, same: c.start())

    zeros5 = jnp.zeros((fields, 128), F32)

    taps_all = w_in.shape[1]
    weights = w_in[...]
    nt = (((1,), (1,)), ((), ()))
    for c in range(3):
        sel = jnp.where(picks((taps_all, 80), 1, 3, c, fields), 1.0, 0.0).astype(BF16)
        wf[16 * c : 16 * c + 16, :] = jnp.dot(weights, sel, preferred_element_type=F32).astype(BF16)
    for b in range(3):
        sel = jnp.where(picks((72, taps_all), 0, 1, 3 * b, fields), 1.0, 0.0).astype(BF16)
        wc[:, 16 * b : 16 * b + 16] = lax.dot_general(
            sel, weights, nt, preferred_element_type=F32
        ).astype(BF16)
    wide_out = jnp.concatenate(
        [w_out[...].astype(F32), jnp.zeros((16 - fields, 16), F32)], axis=0
    ).astype(BF16)
    wo[...] = wide_out
    eye = jnp.where(
        lax.broadcasted_iota(jnp.int32, (16, 16), 0) == lax.broadcasted_iota(jnp.int32, (16, 16), 1),
        1.0, 0.0,
    ).astype(BF16)
    wot[...] = lax.dot_general(eye, wide_out, nt, preferred_element_type=F32).astype(BF16)
    pin_ref[...] = jnp.zeros(pin_ref.shape, F32)
    pout_ref[...] = jnp.zeros(pout_ref.shape, F32)
    gpart[...] = jnp.zeros(gpart.shape, F32)

    def place(b, _):
        def holder(h, found):
            count = jnp.int32(0)
            for j in range(slabs):
                hit = targets[h, j] == p
                at = jnp.logical_and(hit, blocks[h, j] == b)
                found = jnp.where(at, 2 * h + count, found)
                count = count + jnp.where(hit, 1, 0)
            return found

        table[b] = lax.fori_loop(0, slabs, holder, jnp.int32(0))
        return 0

    if slabs <= 16:
        lax.fori_loop(0, slabs, place, 0)

    def blank(slot, recv):
        def one(i, _):
            for n in range(SEC_MOST):
                for y in range(ny):
                    stc[n, i, slot, y] = zeros5
            return 0

        lax.fori_loop(0, sections, one, 0)

        def two(i, _):
            for y in range(ny):
                recv[i, y] = zeros5
            return 0

        lax.fori_loop(0, steps, two, 0)

    @pl.when(jnp.logical_and(active, x == 0))
    def _():
        blank(0, recvm)

    @pl.when(jnp.logical_and(active, x == nx - 1))
    def _():
        blank(2, recvp)

    def a2a_wait(j, _):
        peer = (p + j) % slabs
        rcopy(outgoing.at[p], arrived.at[peer], a2a_s.at[peer], a2a_r.at[peer], t, peer).wait()
        return 0

    lax.fori_loop(1, slabs, a2a_wait, 0)
    keep.wait()

    for b in range(slabs):
        where = jnp.clip((table if slabs <= 16 else given)[b], 0, 2 * slabs - 1)
        holder = where // 2
        rank = where % 2
        for k in range(rows):
            r = b * rows + k
            f, rest = divmod(r, planes * ny)
            xx, y = divmod(rest, ny)
            full[xx, y, pl.ds(f, 1), :] = arrived[holder, rank, pl.ds(k, 1), :]

    def each_init(q, j, action):
        if (q % 2, j) in ((0, 0), (1, 2)):
            return
        xd = p * planes + q + 1 - j

        @pl.when(jnp.logical_and(xd >= 0, xd < nx))
        def _():
            tt, pp = device_of(xd)
            same = jnp.logical_and(tt == t, pp == p)

            @pl.when(jnp.logical_not(same))
            def _():
                action(
                    rcopy(full.at[q], stc.at[0, t, j], init_s.at[q, j], init_r.at[t, j], tt, pp),
                    False,
                )

            @pl.when(same)
            def _():
                action(pltpu.make_async_copy(full.at[q], stc.at[0, t, j], loc.at[2 + j]), True)

    for j in (1, 0, 2):
        for q in range(planes):
            each_init(q, j, lambda c, same: c.start())

    def finish(c, same):
        if same:
            c.wait()
        else:
            c.wait_send()

    lane = lax.broadcasted_iota(jnp.int32, (16, 128), 1)

    def up(v):
        return jnp.where(lane[: v.shape[0]] == 0, 0.0, pltpu.roll(v, 1, 1))

    def down(v):
        return jnp.where(lane[: v.shape[0]] == 127, 0.0, pltpu.roll(v, 127, 1))

    zeros3 = jnp.zeros((8 - fields, 128), F32)
    zeros8 = jnp.zeros((8, 128), F32)

    def pad8(v):
        return jnp.concatenate([v, zeros3], axis=0)

    def lanes(y):
        return slice(y * 128, (y + 1) * 128)

    t_next, p_next = device_of(x + 1)
    t_prev, p_prev = device_of(x + nx - 1 - nx * jnp.where(x > 0, 1, 0))

    def fwd(n, s, way):
        if way == 0:
            return rcopy(stc.at[n, s, 1], stc.at[n, s, 0], fwd_s.at[n - 1, s, 0],
                         fwd_r.at[n - 1, s, 0], t_next, p_next)
        return rcopy(stc.at[n, s, 1], stc.at[n, s, 2], fwd_s.at[n - 1, s, 1],
                     fwd_r.at[n - 1, s, 1], t_prev, p_prev)

    def both(make, action_next, action_prev):
        @pl.when(x < nx - 1)
        def _():
            action_next(make)

        @pl.when(x > 0)
        def _():
            action_prev(make)

    outer = 2 * (p % 2)
    partner = 2 * (p // 2) + 1 - p % 2

    def init_wait(s, j):
        xs = x - 1 + j
        ok = jnp.logical_and(xs >= 0, xs < nx)
        local_one = jnp.logical_and(s == t, (xs + planes) // planes - 1 == p)

        @pl.when(jnp.logical_and(ok, jnp.logical_not(local_one)))
        def _():
            rcopy(full.at[0], stc.at[0, s, j], init_s.at[0, 1], init_r.at[s, j], t, p).wait_recv()

        @pl.when(jnp.logical_and(ok, local_one))
        def _():
            pltpu.make_async_copy(full.at[0], stc.at[0, s, j], loc.at[2 + j]).wait()

    def pass_on(s):
        return rcopy(stc.at[0, s, 1], stc.at[0, s, outer], pair_s.at[s], pair_r.at[s], t, partner)

    def pass_in(s):
        return rcopy(stc.at[0, s, 1], stc.at[0, s, 2 - outer], pair_s.at[s], pair_r.at[s], t, partner)

    def forward(n, s):
        if n == 0:
            init_wait(s, outer)
            pass_in(s).wait_recv()
        else:
            @pl.when(x > 0)
            def _():
                fwd(n, s, 0).wait_recv()

            @pl.when(x < nx - 1)
            def _():
                fwd(n, s, 1).wait_recv()

        def row(a, y):
            if y < 0 or y >= ny:
                return zeros8
            return pad8(stc[n, s, a, y])

        for y in range(ny):
            parts = [row(a, y + b) for a in range(3) for b in (-1, 0, 1)] + [zeros8]
            taps[n, s, :, lanes(y)] = jnp.concatenate(parts, axis=0).astype(BF16)
        u_ref[0:48, :] = jnp.dot(wf[...], taps[n, s], preferred_element_type=F32)
        for y in range(ny):
            u = u_ref[16:32, lanes(y)] + up(u_ref[0:16, lanes(y)]) + down(u_ref[32:48, lanes(y)])
            h = jnp.tanh(u)
            hl[n, s, :, lanes(y)] = h.astype(BF16)
            dh[n, s, :, lanes(y)] = 1.0 - h * h
        last = n == SEC_MOST - 1
        if not last:
            c_ref[0:16, :] = jnp.dot(wo[...], hl[n, s], preferred_element_type=F32)
        for y in range(ny):
            v = row(1, y)
            xm, xp, ym, yp = row(0, y), row(2, y), row(1, y - 1), row(1, y + 1)
            zm, zp = up(v), down(v)
            dx, dy, dz = (xp - xm) * 0.5, (yp - ym) * 0.5, (zp - zm) * 0.5
            pd[n, s, y, 0] = dx * DT
            pd[n, s, y, 1] = dy * DT
            pd[n, s, y, 2] = dz * DT
            if not last:
                lap = xp + xm + yp + ym + zp + zm - 6.0 * v
                adv = v[0:1] * dx + v[1:2] * dy + v[2:3] * dz
                new = v + DT * (lap - adv) + c_ref[0:8, lanes(y)]
                stc[n + 1, s, 1, y] = new[:fields]
        if not last:
            @pl.when(x < nx - 1)
            def _():
                fwd(n + 1, s, 0).start()

            @pl.when(x > 0)
            def _():
                fwd(n + 1, s, 1).start()

    sub = lax.broadcasted_iota(jnp.int32, (8, 128), 0)

    crew = 2 * sections
    bands = slabs // 2
    part = 64 // crew
    seat = 2 * t + p % 2

    def mate(j):
        i = (seat + j) % crew
        return i, i // 2, 2 * (p // 2) + i % 2

    def red1(j):
        i, tt, pp = mate(j)
        return rcopy(gpart.at[i], g1.at[seat], r1_s.at[i], r1_r.at[seat], tt, pp)

    def red1_in(j):
        i, tt, pp = mate(j)
        return rcopy(gpart.at[i], g1.at[i], r1_s.at[i], r1_r.at[i], tt, pp)

    def red2(j):
        i = (p // 2 + j) % bands
        return rcopy(g2, g3.at[p // 2], r2_s.at[i], r2_r.at[p // 2], t, 2 * i + p % 2)

    def red2_in(j):
        i = (p // 2 + j) % bands
        return rcopy(g2, g3.at[i], r2_s.at[i], r2_r.at[i], t, 2 * i + p % 2)

    def red3(j):
        i, tt, pp = mate(j)
        return rcopy(gfin.at[seat], gfin.at[seat], r3_s.at[i], r3_r.at[seat], tt, pp)

    def red3_in(j):
        i, tt, pp = mate(j)
        return rcopy(gfin.at[i], gfin.at[i], r3_s.at[i], r3_r.at[i], tt, pp)

    def band_loop(make, action):
        def one(j, _):
            action(make(j))
            return 0

        lax.fori_loop(1, bands, one, 0)

    def red1_begin():
        for r in range(0, 64, part):
            if r < 48:
                gpart[r // part, :, 0:80] = pin_ref[r : r + part, :]
            else:
                gpart[r // part, :, 0:16] = pout_ref[r - 48 : r - 48 + part, :]
        for j in range(1, crew):
            red1(j).start()
        g1[seat] = gpart[seat]

    def chain(way, k):
        if way == 0:
            return rcopy(sendp.at[k], recvm.at[k], ch_s.at[k, 0], ch_r.at[k, 0], t_next, p_next)
        return rcopy(sendm.at[k], recvp.at[k], ch_s.at[k, 1], ch_r.at[k, 1], t_prev, p_prev)

    @pl.when(active)
    def _():
        def relay(s, _):
            init_wait(s, 1)
            pass_on(s).start()
            return 0

        lax.fori_loop(0, sections, relay, 0)
        for n in range(SEC_MOST):
            def turn(s, _):
                forward(n, s)
                return 0

            lax.fori_loop(0, sections, turn, 0)

        def obs_wait(s, _):
            same = jnp.logical_and(s == t, home == p)

            @pl.when(jnp.logical_not(same))
            def _():
                rcopy(obs.at[0], obsr.at[s], obs_s.at[0], obs_r.at[s], t, p).wait_recv()

            @pl.when(same)
            def _():
                pltpu.make_async_copy(obs.at[0], obsr.at[s], loc.at[1]).wait()

            return 0

        lax.fori_loop(0, sections, obs_wait, 0)

        blp[:, 0:128] = jnp.zeros((16, 128), BF16)
        blp[:, (ny + 1) * 128 :] = jnp.zeros((16, 128), BF16)
        for y in range(ny):
            hist[0, y] = zeros8

        size = [lengths[s] for s in range(sections)]
        after = [None] * sections
        run = jnp.int32(0)
        for s in reversed(range(sections)):
            after[s] = run
            run = run + size[s]

        def step(k, _):
            s = jnp.int32(0)
            for i in range(sections - 1):
                s = s + jnp.where(after[i] > k, 1, 0)
            n = jnp.int32(0)
            begin = jnp.int32(0)
            for i in range(sections):
                n = n + jnp.where(s == i, after[i] + size[i] - 1 - k, 0)
                begin = begin + jnp.where(s == i, after[i], 0)
            n = jnp.clip(n, 0, SEC_MOST - 1)
            first = begin == k
            weight = jnp.where(first, 1.0, 0.0).astype(F32)

            g = []
            for y in range(ny):
                v = hist[k, y] + pad8(obsr[s, y]) * weight
                g.append(v)
                gl[:, lanes(y)] = jnp.concatenate([v, zeros8], axis=0).astype(BF16)
            b32 = jnp.dot(wot[...], gl[...], preferred_element_type=F32) * dh[n, s]
            blp[:, 128 : (ny + 1) * 128] = b32.astype(BF16)
            wide = ny * 128
            stack = jnp.concatenate(
                [blp[:, 256 : 256 + wide], blp[:, 128 : 128 + wide], blp[:, 0:wide]], axis=0
            )
            c_ref[0:24, :] = jnp.dot(wc[0:24, :], stack, preferred_element_type=F32)
            c_ref[48:72, :] = jnp.dot(wc[48:72, :], stack, preferred_element_type=F32)

            def conv(a, c, y):
                return c_ref[(3 * a + c) * 8 : (3 * a + c + 1) * 8, lanes(y)]

            def speed(d, y):
                return stc[n, s, 1, y, pl.ds(d, 1), :]

            for y in range(ny):
                even = g[y] * DT
                m0 = g[y] * (0.5 * DT) * speed(0, y)
                to_next = even - m0 + conv(2, 1, y) + down(conv(2, 0, y)) + up(conv(2, 2, y))
                to_prev = even + m0 + conv(0, 1, y) + down(conv(0, 0, y)) + up(conv(0, 2, y))
                sendp[k, y] = to_next[:fields]
                sendm[k, y] = to_prev[:fields]

            @pl.when(x < nx - 1)
            def _():
                chain(0, k).start()

            @pl.when(x > 0)
            def _():
                chain(1, k).start()

            c_ref[24:48, :] = jnp.dot(wc[24:48, :], stack, preferred_element_type=F32)
            push, pull = [], []
            for y in range(ny):
                half = g[y] * (0.5 * DT)
                even = g[y] * DT
                m1, m2 = half * speed(1, y), half * speed(2, y)
                push.append(even - m1)
                pull.append(even + m1)
                here = g[y] * (1.0 - 6.0 * DT) + conv(1, 1, y)
                here = here + up(even - m2 + conv(1, 2, y)) + down(even + m2 + conv(1, 0, y))
                for d in range(3):
                    term = jnp.sum(g[y] * pd[n, s, y, d], axis=0, keepdims=True)
                    here = here - jnp.where(sub == d, term, 0.0)
                own[y] = here

            base = blp[:, 128 : 128 + wide]
            for y in range(ny):
                r = blp[:, 128 + y * 128 : 256 + y * 128].astype(F32)
                u_ref[0:16, lanes(y)] = down(r)
                u_ref[16:32, lanes(y)] = up(r)
            grads = jnp.concatenate(
                [u_ref[0:16, :].astype(BF16), base, u_ref[16:32, :].astype(BF16)], axis=0
            )
            pin_ref[...] += lax.dot_general(grads, taps[n, s], nt, preferred_element_type=F32)
            pout_ref[...] += lax.dot_general(gl[...], hl[n, s], nt, preferred_element_type=F32)
            for y in range(ny):
                add = own[y]
                if y > 0:
                    add = add + push[y - 1]
                if y < ny - 1:
                    add = add + pull[y + 1]
                own[y] = add

            @pl.when(k == steps - 1)
            def _():
                red1_begin()

            @pl.when(x > 0)
            def _():
                chain(0, k).wait_recv()

            @pl.when(x < nx - 1)
            def _():
                chain(1, k).wait_recv()

            for y in range(ny):
                hist[k + 1, y] = own[y] + pad8(recvm[k, y]) + pad8(recvp[k, y])
            return 0

        lax.fori_loop(0, steps, step, 0)

        for s in range(sections):
            at = jnp.clip(after[s] + size[s], 0, steps)
            for y in range(ny):
                osend[s, y] = hist[at, y][:fields]
        for s in range(sections):
            same = jnp.logical_and(s == t, home == p)

            @pl.when(jnp.logical_not(same))
            def _():
                rcopy(osend.at[s], out_ref.at[spot], out_s.at[s], out_r.at[spot], s, home).start()

            @pl.when(same)
            def _():
                pltpu.make_async_copy(osend.at[s], out_ref.at[spot], loc.at[5]).start()

    @pl.when(jnp.logical_not(active))
    def _():
        red1_begin()

    for j in range(1, crew):
        red1_in(j).wait()
    run1 = g1[0]
    for q in range(1, crew):
        run1 = run1 + g1[q]
    g2[...] = run1
    band_loop(red2, lambda c: c.start())
    g3[p // 2] = run1
    band_loop(red2_in, lambda c: c.wait())
    run2 = g3[0]
    for q in range(1, bands):
        run2 = run2 + g3[q]
    gfin[seat] = run2 * scale
    for j in range(1, crew):
        red3(j).start()

    for q in range(planes):
        tt, pp = device_of(p * planes + q)
        same = jnp.logical_and(tt == t, pp == p)

        @pl.when(jnp.logical_not(same))
        def _():
            rcopy(osend.at[0], out_ref.at[q], out_s.at[0], out_r.at[q], tt, pp).wait_recv()

        @pl.when(same)
        def _():
            pltpu.make_async_copy(osend.at[0], out_ref.at[q], loc.at[5]).wait()

    for q in range(planes):
        each_obs(q, lambda c, same: None if same else c.wait_send())
        for j in range(3):
            each_init(q, j, lambda c, same: None if same else c.wait_send())

    @pl.when(active)
    def _():
        def sent(s, _):
            @pl.when(jnp.logical_not(jnp.logical_and(s == t, home == p)))
            def _():
                rcopy(osend.at[s], out_ref.at[spot], out_s.at[s], out_r.at[spot], s, home).wait_send()

            pass_on(s).wait_send()
            for n in range(1, SEC_MOST):
                @pl.when(x < nx - 1)
                def _():
                    fwd(n, s, 0).wait_send()

                @pl.when(x > 0)
                def _():
                    fwd(n, s, 1).wait_send()

            return 0

        lax.fori_loop(0, sections, sent, 0)

        def sent_chain(k, _):
            @pl.when(x < nx - 1)
            def _():
                chain(0, k).wait_send()

            @pl.when(x > 0)
            def _():
                chain(1, k).wait_send()

            return 0

        lax.fori_loop(0, steps, sent_chain, 0)

    for j in range(1, crew):
        red3_in(j).wait()


def local(ckpt_store, ckpt_target, ckpt_block, lengths, obs_adjoint, w_in, w_out):
    slabs = lax.axis_size("space")
    sections = lax.axis_size("tm")
    observed = obs_adjoint[0]
    fields, planes, ny, depth = observed.shape
    block = ckpt_store.shape[3]
    rows = block // depth
    steps = 2 * sections
    channels = w_in.shape[0]
    grad_scale = 1.0 / math.sqrt(planes * slabs * ny * depth)
    vmem = pl.BlockSpec(memory_space=pltpu.VMEM)
    smem = pl.BlockSpec(memory_space=pltpu.SMEM)

    given = lengths
    if slabs > 16:
        given = pl.pallas_call(
            functools.partial(table_kernel, slabs),
            out_shape=jax.ShapeDtypeStruct((slabs,), jnp.int32),
            in_specs=[smem, smem],
            out_specs=smem,
            name="table",
        )(ckpt_target[0], ckpt_block[0])
    dims = (sections, slabs, planes, ny, fields, rows, steps, grad_scale)
    crew = 2 * sections
    part = 64 // crew
    wide = ny * depth
    face = (ny, fields, depth)
    dma = pltpu.SemaphoreType.DMA
    out, sums = pl.pallas_call(
        functools.partial(main_kernel, dims),
        out_shape=(
            jax.ShapeDtypeStruct((planes,) + face, F32),
            jax.ShapeDtypeStruct((crew, part, depth), F32),
        ),
        in_specs=[vmem, smem, smem, smem, smem, vmem, vmem, vmem],
        out_specs=(vmem, vmem),
        scratch_shapes=[
            pltpu.VMEM((slabs, 2, rows, depth), F32),
            pltpu.VMEM((planes,) + face, F32),
            pltpu.SMEM((slabs,), jnp.int32),
            pltpu.VMEM((slabs, 2, rows, depth), F32),
            pltpu.VMEM((planes,) + face, F32),
            pltpu.VMEM((SEC_MOST, sections, 3) + face, F32),
            pltpu.VMEM((sections,) + face, F32),
            pltpu.VMEM((SEC_MOST, sections, 80, wide), BF16),
            pltpu.VMEM((SEC_MOST, sections, 16, wide), F32),
            pltpu.VMEM((SEC_MOST, sections, 16, wide), BF16),
            pltpu.VMEM((SEC_MOST, sections, ny, 3, 8, depth), F32),
            pltpu.VMEM((16, wide), BF16),
            pltpu.VMEM((16, wide + 2 * depth), BF16),
            pltpu.VMEM((ny, 8, depth), F32),
            pltpu.VMEM((steps + 1, ny, 8, depth), F32),
            pltpu.VMEM((steps,) + face, F32),
            pltpu.VMEM((steps,) + face, F32),
            pltpu.VMEM((steps,) + face, F32),
            pltpu.VMEM((steps,) + face, F32),
            pltpu.VMEM((sections,) + face, F32),
            pltpu.VMEM((64, wide), F32),
            pltpu.VMEM((72, wide), F32),
            pltpu.VMEM((48, 80), BF16),
            pltpu.VMEM((72, 48), BF16),
            pltpu.VMEM((16, 16), BF16),
            pltpu.VMEM((16, 16), BF16),
            pltpu.VMEM((48, 80), F32),
            pltpu.VMEM((16, 16), F32),
            pltpu.VMEM((crew, part, depth), F32),
            pltpu.VMEM((crew, part, depth), F32),
            pltpu.VMEM((part, depth), F32),
            pltpu.VMEM((slabs // 2, part, depth), F32),
            dma((slabs,)), dma((slabs,)),
            dma((planes, 3)), dma((sections, 3)),
            dma((planes,)), dma((sections,)),
            dma((SEC_MOST - 1, sections, 2)), dma((SEC_MOST - 1, sections, 2)),
            dma((steps, 2)), dma((steps, 2)),
            dma((sections,)), dma((planes,)),
            dma((6,)),
            dma((crew,)), dma((crew,)),
            dma((slabs // 2,)), dma((slabs // 2,)),
            dma((crew,)), dma((crew,)),
            dma((sections,)), dma((sections,)),
        ],
        compiler_params=pltpu.CompilerParams(
            collective_id=0, has_side_effects=True, vmem_limit_bytes=56 * 1024 * 1024
        ),
        name="main",
    )(ckpt_store[0, 0], ckpt_target[0], ckpt_block[0], given, lengths, observed, w_in, w_out)

    start_adjoint, grad_in, grad_out = pl.pallas_call(
        finish_kernel,
        out_shape=(
            jax.ShapeDtypeStruct(observed.shape, F32),
            jax.ShapeDtypeStruct(w_in.shape, F32),
            jax.ShapeDtypeStruct(w_out.shape, F32),
        ),
        in_specs=[vmem, vmem],
        out_specs=(vmem, vmem, vmem),
        name="finish",
    )(out, sums.reshape(64, depth))
    return (start_adjoint[None], grad_in, grad_out)


def solution(mesh):
    placed = (
        P("tm", "space", None, None),
        P("tm", None, None),
        P("tm", None, None),
        P(),
        P("tm", None, "space", None, None),
        P(),
        P(),
    )
    return jax.shard_map(
        local,
        mesh=mesh,
        in_specs=placed,
        out_specs=(P("tm", None, "space", None, None), P(), P()),
        check_vma=False,
    )
```

profile of v0, /device:TPU:0, one launch (start us, length us, event | category | flops | bytes accessed | tf_op | source)
XLA Modules:
  0.0 65.5 jit_solution(4608674842053183003)
XLA Ops:
  0.6 63.0 %main.1 = (f32[4,16,5,128]{3,2,1,0:T(8,128)}, f32[8,8,128]{2,1,0:T(8,128)}) custom-call(f32[8,5120]{1,0:T(8,128)} %bitcast.6, s32[8,8]{1,0:T(8,128)} %bitcast.9, s32[8,8]{1,0:T(8,128)} %bitcast.10, s32[4]{0:T(128)} %lengths.1, s32[4]{0:T(128)} %lengths.1, f32[5,4,16,128]{3,2,1,0:T(8,128)} %bitcast.7, bf16[16,135]{1,0:T(8,128)(2,1)} %w_in.1, bf16[5,16]{1,0:T(8,128)(2,1)} %w_out.1), custom_call_target="tpu_custom_call" | custom-call | tf_op jit(solution)/shard_map/main/pallas_call | solution.py:726
  63.6 1.9 %finish.1 = (f32[5,4,16,128]{3,2,1,0:T(8,128)}, f32[16,135]{1,0:T(8,128)}, f32[5,16]{1,0:T(8,128)}) custom-call(f32[4,16,5,128]{3,2,1,0:T(8,128)} %get-tuple-element.8.state_ref, f32[64,128]{1,0:T(8,128)} %bitcast.8), custom_call_target="tpu_custom_call" | custom-call | tf_op jit(solution)/shard_map/finish/pallas_call | solution.py:785
where the time goes:
time: 65.6 us; the launch traced here: 65.5 us
  Pallas kernels  64.8 us (99%)
    pallas_call x1, Pallas kernels, local(): pl.pallas_call(functools.partial(main_kernel, dims), out_shape=(jax.Shape...  63 us
    pallas_call x1, Pallas kernels, local(): pl.pallas_call(finish_kernel, out_shape=(jax.ShapeDtypeStruct(observed.sh...  1.85 us

commit v1 on v0

--- a/solution.py
+++ b/solution.py
@@ -98,24 +98,29 @@
         )
 
     barrier = pltpu.get_barrier_semaphore()
-    total = sections * slabs
-    mine = t * slabs + p
+
+    def hello(there, slab):
+        pl.semaphore_signal(
+            barrier, inc=1, device_id={"tm": there, "space": slab}, device_id_type=MESH
+        )
 
     def greet(j, _):
-        other = (mine + j) % total
-        there, slab = other // slabs, other % slabs
-        gap = slab // 2 - p // 2
-        near = jnp.logical_and(gap >= -1, gap <= 1)
-
-        @pl.when(jnp.logical_or(there == t, near))
-        def _():
-            pl.semaphore_signal(
-                barrier, inc=1, device_id={"tm": there, "space": slab}, device_id_type=MESH
-            )
-
+        hello(t, (p + j) % slabs)
         return 0
 
-    lax.fori_loop(1, total, greet, 0)
+    if slabs <= 16:
+        for j in range(1, slabs):
+            greet(j, 0)
+    else:
+        lax.fori_loop(1, slabs, greet, 0)
+    for gap in (-1, 0, 1):
+        layer = p // 2 + gap
+
+        @pl.when(jnp.logical_and(layer >= 0, layer < slabs // 2))
+        def _():
+            for j in range(1, sections):
+                for c in range(2):
+                    hello((t + j) % sections, 2 * layer + c)
 
     def group(q, _):
         def slot(j, found):
@@ -392,6 +397,7 @@
             pd[n, s, y, 0] = dx * DT
             pd[n, s, y, 1] = dy * DT
             pd[n, s, y, 2] = dz * DT
+            pd[n, s, y, 3] = v
             if not last:
                 lap = xp + xm + yp + ym + zp + zm - 6.0 * v
                 adv = v[0:1] * dx + v[1:2] * dy + v[2:3] * dz
@@ -465,15 +471,16 @@
 
     @pl.when(active)
     def _():
-        def relay(s, _):
+        def relay(i, _):
+            s = sections - 1 - i
             init_wait(s, 1)
             pass_on(s).start()
             return 0
 
         lax.fori_loop(0, sections, relay, 0)
         for n in range(SEC_MOST):
-            def turn(s, _):
-                forward(n, s)
+            def turn(i, _):
+                forward(n, sections - 1 - i)
                 return 0
 
             lax.fori_loop(0, sections, turn, 0)
@@ -536,7 +543,7 @@
                 return c_ref[(3 * a + c) * 8 : (3 * a + c + 1) * 8, lanes(y)]
 
             def speed(d, y):
-                return stc[n, s, 1, y, pl.ds(d, 1), :]
+                return pd[n, s, y, 3, pl.ds(d, 1), :]
 
             for y in range(ny):
                 even = g[y] * DT
@@ -553,6 +560,21 @@
             @pl.when(x > 0)
             def _():
                 chain(1, k).start()
+
+            base = blp[:, 128 : 128 + wide]
+            for y in range(ny):
+                r = blp[:, 128 + y * 128 : 256 + y * 128].astype(F32)
+                u_ref[0:16, lanes(y)] = down(r)
+                u_ref[16:32, lanes(y)] = up(r)
+            grads = jnp.concatenate(
+                [u_ref[0:16, :].astype(BF16), base, u_ref[16:32, :].astype(BF16)], axis=0
+            )
+            pin_ref[...] += lax.dot_general(grads, taps[n, s], nt, preferred_element_type=F32)
+            pout_ref[...] += lax.dot_general(gl[...], hl[n, s], nt, preferred_element_type=F32)
+
+            @pl.when(k == steps - 1)
+            def _():
+                red1_begin()
 
             c_ref[24:48, :] = jnp.dot(wc[24:48, :], stack, preferred_element_type=F32)
             push, pull = [], []
@@ -569,16 +591,6 @@
                     here = here - jnp.where(sub == d, term, 0.0)
                 own[y] = here
 
-            base = blp[:, 128 : 128 + wide]
-            for y in range(ny):
-                r = blp[:, 128 + y * 128 : 256 + y * 128].astype(F32)
-                u_ref[0:16, lanes(y)] = down(r)
-                u_ref[16:32, lanes(y)] = up(r)
-            grads = jnp.concatenate(
-                [u_ref[0:16, :].astype(BF16), base, u_ref[16:32, :].astype(BF16)], axis=0
-            )
-            pin_ref[...] += lax.dot_general(grads, taps[n, s], nt, preferred_element_type=F32)
-            pout_ref[...] += lax.dot_general(gl[...], hl[n, s], nt, preferred_element_type=F32)
             for y in range(ny):
                 add = own[y]
                 if y > 0:
@@ -586,10 +598,6 @@
                 if y < ny - 1:
                     add = add + pull[y + 1]
                 own[y] = add
-
-            @pl.when(k == steps - 1)
-            def _():
-                red1_begin()
 
             @pl.when(x > 0)
             def _():
@@ -742,7 +750,7 @@
             pltpu.VMEM((SEC_MOST, sections, 80, wide), BF16),
             pltpu.VMEM((SEC_MOST, sections, 16, wide), F32),
             pltpu.VMEM((SEC_MOST, sections, 16, wide), BF16),
-            pltpu.VMEM((SEC_MOST, sections, ny, 3, 8, depth), F32),
+            pltpu.VMEM((SEC_MOST, sections, ny, 4, 8, depth), F32),
             pltpu.VMEM((16, wide), BF16),
             pltpu.VMEM((16, wide + 2 * depth), BF16),
             pltpu.VMEM((ny, 8, depth), F32),

time: 65.6 us -> 65.4 us (level)
  no operation moved by 1% of the time
where the time goes in v1:
time: 65.4 us; the launch traced here: 65.3 us
  Pallas kernels  64.7 us (99%)
    pallas_call x1, Pallas kernels, local(): pl.pallas_call(functools.partial(main_kernel, dims), out_shape=(jax.Shape...  62.8 us
    pallas_call x1, Pallas kernels, local(): pl.pallas_call(finish_kernel, out_shape=(jax.ShapeDtypeStruct(observed.sh...  1.85 us

profile of v1, /device:TPU:0, one launch (start us, length us, event | category | flops | bytes accessed | tf_op | source)
XLA Modules:
  0.0 65.3 jit_solution(13582586328314730473)
XLA Ops:
  0.6 62.8 %main.1 = (f32[4,16,5,128]{3,2,1,0:T(8,128)}, f32[8,8,128]{2,1,0:T(8,128)}) custom-call(f32[8,5120]{1,0:T(8,128)} %bitcast.6, s32[8,8]{1,0:T(8,128)} %bitcast.9, s32[8,8]{1,0:T(8,128)} %bitcast.10, s32[4]{0:T(128)} %lengths.1, s32[4]{0:T(128)} %lengths.1, f32[5,4,16,128]{3,2,1,0:T(8,128)} %bitcast.7, bf16[16,135]{1,0:T(8,128)(2,1)} %w_in.1, bf16[5,16]{1,0:T(8,128)(2,1)} %w_out.1), custom_call_target="tpu_custom_call" | custom-call | tf_op jit(solution)/shard_map/main/pallas_call | solution.py:734
  63.4 1.9 %finish.1 = (f32[5,4,16,128]{3,2,1,0:T(8,128)}, f32[16,135]{1,0:T(8,128)}, f32[5,16]{1,0:T(8,128)}) custom-call(f32[4,16,5,128]{3,2,1,0:T(8,128)} %get-tuple-element.8.state_ref, f32[64,128]{1,0:T(8,128)} %bitcast.8), custom_call_target="tpu_custom_call" | custom-call | tf_op jit(solution)/shard_map/finish/pallas_call | solution.py:793

commit v2 on v1

--- a/solution.py
+++ b/solution.py
@@ -483,7 +483,7 @@
                 forward(n, sections - 1 - i)
                 return 0
 
-            lax.fori_loop(0, sections, turn, 0)
+            lax.fori_loop(0, sections if n < SEC_MOST - 1 else 1, turn, 0)
 
         def obs_wait(s, _):
             same = jnp.logical_and(s == t, home == p)
@@ -598,6 +598,11 @@
                 if y < ny - 1:
                     add = add + pull[y + 1]
                 own[y] = add
+
+            for i in range(sections - 1):
+                @pl.when(k == i)
+                def _():
+                    forward(SEC_MOST - 1, sections - 2 - i)
 
             @pl.when(x > 0)
             def _():

time: 65.4 us -> 64.1 us (0.980)
  Pallas kernels: 64.7 us -> 63.3 us
    pallas_call x1, Pallas kernels: 62.8 us -> 61.4 us  [local(): pl.pallas_call(functools.partial(main_kernel, dims), out_shape=(jax.Shape...]
where the time goes in v2:
time: 64.1 us; the launch traced here: 63.9 us
  Pallas kernels  63.3 us (99%)
    pallas_call x1, Pallas kernels, local(): pl.pallas_call(functools.partial(main_kernel, dims), out_shape=(jax.Shape...  61.4 us
    pallas_call x1, Pallas kernels, local(): pl.pallas_call(finish_kernel, out_shape=(jax.ShapeDtypeStruct(observed.sh...  1.85 us

profile of v2, /device:TPU:0, one launch (start us, length us, event | category | flops | bytes accessed | tf_op | source)
XLA Modules:
  0.0 63.9 jit_solution(14422453886296860304)
XLA Ops:
  0.6 61.4 %main.1 = (f32[4,16,5,128]{3,2,1,0:T(8,128)}, f32[8,8,128]{2,1,0:T(8,128)}) custom-call(f32[8,5120]{1,0:T(8,128)} %bitcast.6, s32[8,8]{1,0:T(8,128)} %bitcast.9, s32[8,8]{1,0:T(8,128)} %bitcast.10, s32[4]{0:T(128)} %lengths.1, s32[4]{0:T(128)} %lengths.1, f32[5,4,16,128]{3,2,1,0:T(8,128)} %bitcast.7, bf16[16,135]{1,0:T(8,128)(2,1)} %w_in.1, bf16[5,16]{1,0:T(8,128)(2,1)} %w_out.1), custom_call_target="tpu_custom_call" | custom-call | tf_op jit(solution)/shard_map/main/pallas_call | solution.py:739
  62.1 1.9 %finish.1 = (f32[5,4,16,128]{3,2,1,0:T(8,128)}, f32[16,135]{1,0:T(8,128)}, f32[5,16]{1,0:T(8,128)}) custom-call(f32[4,16,5,128]{3,2,1,0:T(8,128)} %get-tuple-element.8.state_ref, f32[64,128]{1,0:T(8,128)} %bitcast.8), custom_call_target="tpu_custom_call" | custom-call | tf_op jit(solution)/shard_map/finish/pallas_call | solution.py:798
